TPU v7x, 32 devices: a whole 2x2x4 slice. The times are simulated.
32 devices in a mesh: ens: 2 (over y), hist: 4 (over z), mom: 2 (over x), rep: 2 (over core).
Axes of the slice: x: 2, y: 2, z: 4, core: 2. Of those that a mesh axis runs over, the one named last changes fastest.
Arguments:
- history_stat: float32 [512, 1024, 512], P(('hist', 'rep'), 'ens', 'mom'), parts along dimension 1, may hold values from -6 to 6, as said below
- history_spec: float32 [512, 1024, 512], P(('hist', 'rep'), 'ens', 'mom'), parts along dimension 1, may hold values from -6 to 6, as said below
Outputs:
- rows_stat: float32 [6, 512, 512], P('ens', ('hist', 'rep'), 'mom'), parts along dimension 0
- rows_spec: float32 [6, 512, 512], P('ens', ('hist', 'rep'), 'mom'), parts along dimension 0
- newest_stat: float32 [10, 5, 512], P('ens', None, 'mom'), parts along dimension 0
- newest_spec: float32 [10, 5, 512], P('ens', None, 'mom'), parts along dimension 0
There are 2 independent parts, one for each index of `ens`. A program takes and returns all parts, laid end to end along the dimension named above; each array names one. Nothing has to cross between parts.
Inputs may be any that keep to these rules, and one draw needn't show every extreme that they name: `history_stat`: symmetric under exchange of its two time indices. `history_spec`: antisymmetric under exchange of its two time indices, zero where they are equal.
All inputs are finite; a program needn't handle non-finite values.
Results may differ from a plain program's by a relative error of at most 0.0003.
Values sent between devices are 32-bit elements; how exact they have to be, the bound alone decides.
A program may use at most 128 MiB of HBM per device.

v0:
```python
import functools
import math

import jax
import jax.numpy as jnp
import ml_dtypes
import numpy as np
from jax import lax
from jax.experimental import pallas as pl
from jax.experimental.pallas import tpu as pltpu
from jax.sharding import PartitionSpec as P

STEPS = 3
TIME_STEP = 0.12
CUTOFF = 12.8
MASS_SQUARED = 1.0
SUNSET_COUPLING = 100.0
HARTREE_COUPLING = 2.45
MESH = pl.DeviceIdType.MESH
LANES = 128
TILE = 8
ROWS_AT_ONCE = 4
SLOTS = 3
RESIDENT_BYTES = 48 << 20
F32 = jnp.float32
BF16 = jnp.bfloat16


def sine_table(points):
    index = np.arange(1, points + 1, dtype=np.int64)
    product = index[:, None] * index[None, :] % (2 * (points + 1))
    table = np.sin(product.astype(np.float64) * (math.pi / (points + 1)))
    high = table.astype(np.float32).astype(ml_dtypes.bfloat16)
    low = (table - high.astype(np.float64)).astype(np.float32).astype(ml_dtypes.bfloat16)
    return high, low


def split(value):
    high = value.astype(BF16)
    low = (value - high.astype(F32)).astype(BF16)
    return high, low


def dot3(value, high_table, low_table):
    high, low = split(value)
    out = jnp.dot(high, high_table, preferred_element_type=F32)
    out += jnp.dot(low, high_table, preferred_element_type=F32)
    return out + jnp.dot(high, low_table, preferred_element_type=F32)


def kernel(
    sizes,
    hist_stat, hist_spec, sine_high_hbm, sine_low_hbm,
    rows_stat, rows_spec, newest_stat, newest_spec,
    sine_high, sine_low, keep, stream, gathered, swap, columns, acc_a, acc_bc, first_cols,
    table_sem, col_sem, keep_sem, stream_sem, swap_send, swap_recv, send_sem, recv_sem,
):
    z_count, m_count, c_count, rows, times, width, kept = sizes
    points = m_count * width
    groups = z_count * c_count
    streamed = rows - kept
    z, m, c = lax.axis_index("hist"), lax.axis_index("mom"), lax.axis_index("rep")
    me = z * c_count + c
    last = groups - 1
    chunks = ((0, rows), (rows, rows + 2 * TILE))
    near = jnp.minimum(z, z_count - 1 - z)

    def source(n):
        paired = n <= 2 * near
        step = jnp.where(paired, (n + 1) // 2, n - near)
        below = jnp.where(paired, n % 2 == 1, 2 * z > z_count - 1)
        return jnp.where(below, z - step, z + step), below

    def group_of(q):
        return source(q // c_count)[0] * c_count + (c + q % c_count) % c_count

    tables = [
        pltpu.make_async_copy(sine_high_hbm, sine_high, table_sem.at[0]),
        pltpu.make_async_copy(sine_low_hbm, sine_low, table_sem.at[1]),
    ]
    cols = [
        pltpu.make_async_copy(h.at[:, pl.ds(times - TILE, TILE), :], first_cols.at[k], col_sem.at[k])
        for k, h in enumerate((hist_stat, hist_spec))
    ]
    for copy in cols + tables:
        copy.start()

    def keep_copies(q):
        part = pl.ds(pl.multiple_of(group_of(q) * rows, TILE), rows)
        return [
            pltpu.make_async_copy(
                h.at[pl.ds(0, kept), part, :], keep.at[k, :, part, :], keep_sem.at[q, k]
            )
            for k, h in enumerate((hist_stat, hist_spec))
        ]

    def stream_copies(total):
        part = pl.ds(pl.multiple_of(group_of(total % groups) * rows, TILE), rows)
        slot = total % SLOTS
        return [
            pltpu.make_async_copy(
                h.at[pl.ds(kept, streamed), part, :], stream.at[slot, k], stream_sem.at[slot, k]
            )
            for k, h in enumerate((hist_stat, hist_spec))
        ]

    barrier = pltpu.get_barrier_semaphore()
    for k in range(1, m_count):
        pl.semaphore_signal(barrier, inc=1, device_id={"mom": (m + k) % m_count}, device_id_type=MESH)
    for k in range(1, c_count):
        pl.semaphore_signal(barrier, inc=1, device_id={"rep": (c + k) % c_count}, device_id_type=MESH)

    @pl.when(z > 0)
    def _():
        pl.semaphore_signal(barrier, inc=1, device_id={"hist": z - 1}, device_id_type=MESH)

    @pl.when(z < z_count - 1)
    def _():
        pl.semaphore_signal(barrier, inc=1, device_id={"hist": z + 1}, device_id_type=MESH)

    for copy in cols:
        copy.wait()

    @pl.loop(0, groups)
    def _(q):
        for copy in keep_copies(q):
            copy.start()
        if streamed:
            @pl.when(q < SLOTS)
            def _():
                for copy in stream_copies(q):
                    copy.start()

    columns[0, 0] = first_cols[0, :, TILE - 2, :]
    columns[0, 1] = first_cols[0, :, TILE - 1, :]
    columns[1, 0] = -first_cols[1, :, TILE - 2, :]
    columns[1, 1] = -first_cols[1, :, TILE - 1, :]
    outs = (rows_stat, rows_spec)

    def column(k, a):
        return columns[k, a] if a < 2 else outs[k][a - 2]

    along = jnp.where(z > 0, 1, 0) + jnp.where(z < z_count - 1, 1, 0)
    pl.semaphore_wait(barrier, m_count - 1 + c_count - 1 + along)

    dp = CUTOFF / points
    dr = math.pi / ((points + 1) * dp)
    every = lax.broadcasted_iota(jnp.int32, (1, points), 1).astype(F32) + 1.0
    radius = every * dr
    inverse_radius = 1.0 / radius
    back_factor = (4.0 * math.pi * dr) * radius
    lane = lax.broadcasted_iota(jnp.int32, (1, width), 1)
    momentum = ((lane + m * width).astype(F32) + 1.0) * dp
    inverse_momentum = 1.0 / momentum

    def momenta_of(part):
        return ((lane + part * width).astype(F32) + 1.0) * dp

    row_time = me * rows + lax.broadcasted_iota(jnp.int32, (rows, 1), 0)
    is_last = (me == last).astype(F32)
    factor = TIME_STEP * TIME_STEP
    extended = rows + TILE
    own_part = pl.ds(pl.multiple_of(m * width, LANES), width)
    zero_row = jnp.zeros((1, width), F32)
    block_stat, block_spec = {}, {}
    inner = lax.broadcasted_iota(jnp.int32, (rows, LANES), 0)

    def fold(value):
        return jnp.sum(value.reshape(rows // TILE, TILE, LANES), axis=0)

    def send(s, group, chunk, way, target):
        start, size = chunks[chunk]
        view = gathered.at[s, group, pl.ds(start, size), :]
        return pltpu.make_async_remote_copy(
            src_ref=view,
            dst_ref=view,
            send_sem=send_sem.at[group, chunk, way],
            recv_sem=recv_sem.at[s, group, chunk],
            device_id=target,
            device_id_type=MESH,
        )

    for s in range(STEPS):
        current = s + 1
        for k in range(2):
            blocks = (block_stat, block_spec)[k]
            swap[s, m, k, pl.ds(0, rows), :] = column(k, current)
            extra = [
                blocks[(current, a)] if 2 <= a <= current else zero_row for a in range(TILE)
            ]
            swap[s, m, k, pl.ds(rows, TILE), :] = jnp.concatenate(extra, axis=0)
        swaps = []
        for k in range(1, m_count):
            to = (m + k) % m_count
            copy = pltpu.make_async_remote_copy(
                src_ref=swap.at[s, m],
                dst_ref=swap.at[s, m],
                send_sem=swap_send.at[s, k],
                recv_sem=swap_recv.at[s, k],
                device_id={"mom": to},
                device_id_type=MESH,
            )
            copy.start()
            swaps.append(copy)
        if s == 0:
            for copy in tables:
                copy.wait()

        tadpole_row = rows - 1 if s == 0 else rows + current
        radial = None
        tadpole = None
        for k in range(m_count):
            part = (m - k + m_count) % m_count
            if k:
                swaps[k - 1].wait_recv()
            momenta = momenta_of(part)
            weight = momenta * (dp / (2.0 * math.pi**2))
            value = swap[s, part].reshape(2 * extended, width)
            span = pl.ds(pl.multiple_of(part * width, LANES), width)
            term = dot3(value * weight, sine_high[span, :], sine_low[span, :])
            radial = term if radial is None else radial + term
            line = swap[s, part, 0, pl.ds(tadpole_row, 1), :]
            term = jnp.sum(weight * momenta * line, axis=1, keepdims=True)
            tadpole = term if tadpole is None else tadpole + term
        field_stat = radial[:extended] * inverse_radius
        field_spec = radial[extended:] * inverse_radius
        square_stat, square_spec = field_stat * field_stat, field_spec * field_spec
        sigma_stat = -SUNSET_COUPLING * field_stat * (square_stat - 0.75 * square_spec)
        sigma_spec = -SUNSET_COUPLING * field_spec * (3.0 * square_stat - 0.25 * square_spec)
        sigma = jnp.concatenate([sigma_stat * back_factor, sigma_spec * back_factor], axis=0)
        sigma = dot3(sigma, sine_high[:, own_part], sine_low[:, own_part]) * inverse_momentum
        group_stat, group_spec = sigma[:rows], sigma[extended : extended + rows]
        new_stat, new_spec = sigma[rows:extended], sigma[extended + rows :]

        gathered[s, me, pl.ds(0, rows), :] = group_stat
        extra = []
        for a in range(5):
            if a > current:
                extra.append(zero_row)
                continue
            spec = column(1, a)
            if a < 2:
                spec = jnp.where(row_time <= times - 2 + a, spec, 0.0)
            value = group_spec * column(0, a) + group_stat * spec
            extra.append(-jnp.sum(value, axis=0, keepdims=True))
        for a in range(2):
            spec = jnp.where(row_time >= times - 2 + a, column(1, a), 0.0)
            extra.append(jnp.sum(group_spec * spec, axis=0, keepdims=True))
        extra.append(jnp.broadcast_to(tadpole * is_last, (1, width)))
        for k in range(2):
            for b in range(2):
                for a in range(2):
                    corner = columns[k, a, pl.ds(rows - 2 + b, 1), :]
                    extra.append((is_last if k == 0 else -is_last) * corner)
        gathered[s, me, pl.ds(rows, rows + 2 * TILE), :] = jnp.concatenate([group_spec] + extra, axis=0)
        for chunk in range(2):
            @pl.when(z > 0)
            def _():
                send(s, me, chunk, 0, {"hist": z - 1}).start()

            @pl.when(z < z_count - 1)
            def _():
                send(s, me, chunk, 1, {"hist": z + 1}).start()

            for k in range(1, c_count):
                send(s, me, chunk, 1 + k, {"rep": (c + k) % c_count}).start()

        def add_block(q, first):
            group = group_of(q)
            total = s * groups + q
            part = pl.ds(pl.multiple_of(group * rows, TILE), rows)
            if s == 0:
                for copy in keep_copies(q):
                    copy.wait()
            if streamed:
                for copy in stream_copies(total):
                    copy.wait()
            earlier = group < me
            target = jnp.where(earlier, 0, 1)
            for t in range(width // LANES):
                lanes = pl.ds(t * LANES, LANES)
                sig_stat = gathered[s, group, pl.ds(0, rows), lanes]
                sig_spec = gathered[s, group, pl.ds(rows, rows), lanes]
                mixed = sig_spec if first else jnp.where(earlier, sig_stat, sig_spec)

                def body(i, f, r):
                    a = fold(sig_spec * f)
                    if first:
                        acc_a[i, :, lanes] = a
                        acc_bc[0, i, :, lanes] = fold(jnp.where(inner < i, sig_stat, 0.0) * r)
                        acc_bc[1, i, :, lanes] = fold(jnp.where(inner > i, sig_spec, 0.0) * r)
                    else:
                        acc_a[i, :, lanes] += a
                        acc_bc[target, i, :, lanes] += fold(mixed * r)

                @pl.loop(0, kept // ROWS_AT_ONCE)
                def _(b):
                    for u in range(ROWS_AT_ONCE):
                        i = b * ROWS_AT_ONCE + u
                        body(i, keep[0, i, part, lanes], keep[1, i, part, lanes])

                if streamed:
                    slot = total % SLOTS

                    @pl.loop(0, streamed // ROWS_AT_ONCE)
                    def _(b):
                        for u in range(ROWS_AT_ONCE):
                            i = b * ROWS_AT_ONCE + u
                            body(kept + i, stream[slot, 0, i, :, lanes], stream[slot, 1, i, :, lanes])

            if streamed:
                @pl.when(total + SLOTS < STEPS * groups)
                def _():
                    for copy in stream_copies(total + SLOTS):
                        copy.start()

        def from_others(n):
            zz, below = source(n)
            for k in range(1, c_count):
                group = zz * c_count + (c - k + c_count) % c_count
                for chunk in range(2):
                    send(s, group, chunk, 1 + k, {"rep": (c + k) % c_count}).wait_recv()

        add_block(0, True)
        from_others(0)
        for j in range(1, c_count):
            add_block(j, False)

        @pl.loop(1, z_count)
        def _(n):
            zz, below = source(n)
            group = zz * c_count + c
            for chunk in range(2):
                send(s, group, chunk, 0, {"hist": z}).wait_recv()

                @pl.when(below & (z < z_count - 1))
                def _():
                    send(s, group, chunk, 1, {"hist": z + 1}).start()

                @pl.when(jnp.logical_not(below) & (z > 0))
                def _():
                    send(s, group, chunk, 0, {"hist": z - 1}).start()

                for k in range(1, c_count):
                    send(s, group, chunk, 1 + k, {"rep": (c + k) % c_count}).start()
            add_block(n * c_count, False)
            from_others(n)
            for j in range(1, c_count):
                add_block(n * c_count + j, False)

        total = jnp.sum(gathered[s, :, pl.ds(2 * rows, 2 * TILE), :], axis=0)

        def total_row(i):
            return total[i : i + 1]

        if s == 0:
            for b in range(2):
                for a in range(2):
                    block_stat[(b, a)] = total_row(8 + 2 * b + a)
                    block_spec[(b, a)] = total_row(12 + 2 * b + a)
        frequency = momentum * momentum + MASS_SQUARED + HARTREE_COUPLING * total_row(7)

        memory_stat = -(jnp.sum(acc_a[...], axis=1) + jnp.sum(acc_bc[0], axis=1))
        memory_spec = jnp.sum(acc_bc[1], axis=1)
        for b in range(2, current + 1):
            weight = new_spec[b : b + 1]
            memory_stat = memory_stat - weight * column(0, b)
            memory_spec = memory_spec - weight * column(1, b)
        for k, memory in enumerate((memory_stat, memory_spec)):
            now = column(k, current)
            outs[k][s] = 2.0 * now - column(k, s) - factor * (frequency * now + TIME_STEP * memory)

        line_stat, line_spec = [], []
        for a in range(current + 1):
            m_stat = total_row(a)
            m_spec = total_row(5 + a) if a < 2 else zero_row
            for b in range(2, current + 1):
                m_stat = m_stat - new_spec[b : b + 1] * block_stat[(b, a)]
                if b <= a:
                    m_stat = m_stat + new_stat[b : b + 1] * block_spec[(b, a)]
                if b >= a:
                    m_spec = m_spec - new_spec[b : b + 1] * block_spec[(b, a)]
            now = block_stat[(current, a)]
            line_stat.append(
                2.0 * now - block_stat[(s, a)] - factor * (frequency * now + TIME_STEP * m_stat)
            )
            now = block_spec[(current, a)]
            line_spec.append(
                2.0 * now - block_spec[(s, a)] - factor * (frequency * now + TIME_STEP * m_spec)
            )
            newest_memory = m_stat
        line_stat.append(
            2.0 * line_stat[current]
            - line_stat[s]
            - factor * (frequency * line_stat[current] + TIME_STEP * newest_memory)
        )
        line_spec.append(zero_row)
        for a in range(current + 2):
            block_stat[(a, current + 1)] = line_stat[a]
            block_stat[(current + 1, a)] = line_stat[a]
            block_spec[(a, current + 1)] = -line_spec[a]
            block_spec[(current + 1, a)] = line_spec[a]

        for copy in swaps:
            copy.wait_send()

        @pl.loop(0, z_count)
        def _(n):
            zz, below = source(n)
            group = zz * c_count + c
            for chunk in range(2):
                @pl.when(((n == 0) | below) & (z < z_count - 1))
                def _():
                    send(s, group, chunk, 1, {"hist": z + 1}).wait_send()

                @pl.when(((n == 0) | jnp.logical_not(below)) & (z > 0))
                def _():
                    send(s, group, chunk, 0, {"hist": z - 1}).wait_send()

                for k in range(1, c_count):
                    send(s, group, chunk, 1 + k, {"rep": (c + k) % c_count}).wait_send()

    for a in range(STEPS + 2):
        for b in range(STEPS + 2):
            newest_stat[a, pl.ds(b, 1), :] = block_stat[(a, b)]
            newest_spec[a, pl.ds(b, 1), :] = block_spec[(a, b)]


def shards(history_stat, history_spec):
    rows, times, width = history_stat.shape
    z_count, m_count, c_count = (lax.axis_size(a) for a in ("hist", "mom", "rep"))
    groups = z_count * c_count
    points = m_count * width
    newest = STEPS + 2
    row_bytes = 2 * times * width * 4
    kept = min(rows, RESIDENT_BYTES // row_bytes // TILE * TILE)
    streamed = rows - kept
    high, low = sine_table(points)
    sizes = (z_count, m_count, c_count, rows, times, width, kept)
    any_spec = pl.BlockSpec(memory_space=pl.ANY)
    vmem = pl.BlockSpec(memory_space=pltpu.VMEM)
    dma = pltpu.SemaphoreType.DMA
    stream_rows = max(streamed, TILE)
    stream_cols = rows if streamed else TILE
    return pl.pallas_call(
        functools.partial(kernel, sizes),
        out_shape=(
            jax.ShapeDtypeStruct((STEPS, rows, width), F32),
            jax.ShapeDtypeStruct((STEPS, rows, width), F32),
            jax.ShapeDtypeStruct((newest, newest, width), F32),
            jax.ShapeDtypeStruct((newest, newest, width), F32),
        ),
        in_specs=[any_spec] * 4,
        out_specs=(vmem,) * 4,
        scratch_shapes=[
            pltpu.VMEM((points, points), BF16),
            pltpu.VMEM((points, points), BF16),
            pltpu.VMEM((2, kept, times, width), F32),
            pltpu.VMEM((SLOTS, 2, stream_rows, stream_cols, width), F32),
            pltpu.VMEM((STEPS, groups, 2 * rows + 2 * TILE, width), F32),
            pltpu.VMEM((STEPS, m_count, 2, rows + TILE, width), F32),
            pltpu.VMEM((2, 2, rows, width), F32),
            pltpu.VMEM((rows, TILE, width), F32),
            pltpu.VMEM((2, rows, TILE, width), F32),
            pltpu.VMEM((2, rows, TILE, width), F32),
            dma((2,)),
            dma((2,)),
            dma((groups, 2)),
            dma((SLOTS, 2)),
            dma((STEPS, m_count)),
            dma((STEPS, m_count)),
            dma((groups, 2, 1 + c_count)),
            dma((STEPS, groups, 2)),
        ],
        compiler_params=pltpu.CompilerParams(
            collective_id=0, has_side_effects=True, vmem_limit_bytes=67043328
        ),
        name="steps",
    )(history_stat, history_spec, jnp.asarray(high), jnp.asarray(low))


def solution(mesh):
    in_specs = (P(("hist", "rep"), "ens", "mom"), P(("hist", "rep"), "ens", "mom"))
    out_specs = (
        P("ens", ("hist", "rep"), "mom"),
        P("ens", ("hist", "rep"), "mom"),
        P("ens", None, "mom"),
        P("ens", None, "mom"),
    )
    return jax.shard_map(shards, mesh=mesh, in_specs=in_specs, out_specs=out_specs, check_vma=False)
```

profile of v0, /device:TPU:0, one launch (start us, length us, event | category | flops | bytes accessed | tf_op | source)
XLA Modules:
  0.0 89.8 jit_solution(4412124912415979612)
XLA Ops:
  0.6 83.2 %steps.1 = (f32[3,64,256]{2,1,0:T(8,128)}, f32[3,64,256]{2,1,0:T(8,128)}, f32[5,5,256]{2,1,0:T(8,128)}, f32[5,5,256]{2,1,0:T(8,128)}) custom-call(f32[64,512,256]{2,1,0:T(8,128)} %hist_stat.1, f32[64,512,256]{2,1,0:T(8,128)} %hist_spec.1, bf16[512,512]{1,0:T(8,128)(2,1)} %constant.4.clone.sine_high_hbm, bf16[512,512]{1,0:T(8,128)(2,1)} %constant.5.clone.sine_low_hbm), custom_call_target="tpu_custom_call" | custom-call | tf_op jit(solution)/shard_map/steps/pallas_call | solution.py:445
  83.8 1.6 %copy.12 = f32[3,64,256]{2,1,0:T(8,128)} copy(f32[3,64,256]{2,1,0:T(8,128)} %get-tuple-element.8) | data formatting | bytes 393216
  85.4 1.6 %copy.13 = f32[3,64,256]{2,1,0:T(8,128)} copy(f32[3,64,256]{2,1,0:T(8,128)} %get-tuple-element.9) | data formatting | bytes 393216
  87.0 1.4 %copy.14 = f32[5,5,256]{2,1,0:T(8,128)} copy(f32[5,5,256]{2,1,0:T(8,128)} %get-tuple-element.10) | data formatting | bytes 51200
  88.4 1.4 %copy.15 = f32[5,5,256]{2,1,0:T(8,128)} copy(f32[5,5,256]{2,1,0:T(8,128)} %get-tuple-element.11) | data formatting | bytes 51200
where the time goes:
time: 90.2 us; the launch traced here: 89.8 us
  Pallas kernels  83.2 us (92%)
  local copies, waits for them, and re-layouts  6.03 us (7%)
    pallas_call x1, Pallas kernels, shards(): pl.pallas_call(functools.partial(kernel, sizes), out_shape=(jax.ShapeDtyp...  83.2 us
    unnamed x4, local copies, waits for them, and re-layouts  6.03 us

commit v1 on v0

--- a/solution.py
+++ b/solution.py
@@ -62,7 +62,7 @@
     z, m, c = lax.axis_index("hist"), lax.axis_index("mom"), lax.axis_index("rep")
     me = z * c_count + c
     last = groups - 1
-    chunks = ((0, rows), (rows, rows + 2 * TILE))
+    half = rows // 2
     near = jnp.minimum(z, z_count - 1 - z)
 
     def source(n):
@@ -118,9 +118,6 @@
     def _():
         pl.semaphore_signal(barrier, inc=1, device_id={"hist": z + 1}, device_id_type=MESH)
 
-    for copy in cols:
-        copy.wait()
-
     @pl.loop(0, groups)
     def _(q):
         for copy in keep_copies(q):
@@ -131,6 +128,8 @@
                 for copy in stream_copies(q):
                     copy.start()
 
+    for copy in cols:
+        copy.wait()
     columns[0, 0] = first_cols[0, :, TILE - 2, :]
     columns[0, 1] = first_cols[0, :, TILE - 1, :]
     columns[1, 0] = -first_cols[1, :, TILE - 2, :]
@@ -169,7 +168,8 @@
         return jnp.sum(value.reshape(rows // TILE, TILE, LANES), axis=0)
 
     def send(s, group, chunk, way, target):
-        start, size = chunks[chunk]
+        start = chunk * rows
+        size = rows + (0 if chunk == 0 else 2 * TILE if s == 0 else TILE)
         view = gathered.at[s, group, pl.ds(start, size), :]
         return pltpu.make_async_remote_copy(
             src_ref=view,
@@ -180,6 +180,23 @@
             device_id_type=MESH,
         )
 
+    def drain(s):
+        @pl.loop(0, z_count)
+        def _(n):
+            zz, below = source(n)
+            group = zz * c_count + c
+            for chunk in range(2):
+                @pl.when(((n == 0) | below) & (z < z_count - 1))
+                def _():
+                    send(s, group, chunk, 1, {"hist": z + 1}).wait_send()
+
+                @pl.when(((n == 0) | jnp.logical_not(below)) & (z > 0))
+                def _():
+                    send(s, group, chunk, 0, {"hist": z - 1}).wait_send()
+
+                for k in range(1, c_count):
+                    send(s, group, chunk, 1 + k, {"rep": (c + k) % c_count}).wait_send()
+
     for s in range(STEPS):
         current = s + 1
         for k in range(2):
@@ -189,81 +206,94 @@
                 blocks[(current, a)] if 2 <= a <= current else zero_row for a in range(TILE)
             ]
             swap[s, m, k, pl.ds(rows, TILE), :] = jnp.concatenate(extra, axis=0)
+        pieces = ((0, half), (half, half + TILE))
         swaps = []
-        for k in range(1, m_count):
-            to = (m + k) % m_count
-            copy = pltpu.make_async_remote_copy(
-                src_ref=swap.at[s, m],
-                dst_ref=swap.at[s, m],
-                send_sem=swap_send.at[s, k],
-                recv_sem=swap_recv.at[s, k],
-                device_id={"mom": to},
-                device_id_type=MESH,
-            )
-            copy.start()
-            swaps.append(copy)
+        for start, size in pieces:
+            for k in range(1, m_count):
+                view = swap.at[s, m, :, pl.ds(start, size), :]
+                copy = pltpu.make_async_remote_copy(
+                    src_ref=view,
+                    dst_ref=view,
+                    send_sem=swap_send.at[s, len(swaps)],
+                    recv_sem=swap_recv.at[s, len(swaps)],
+                    device_id={"mom": (m + k) % m_count},
+                    device_id_type=MESH,
+                )
+                copy.start()
+                swaps.append(copy)
         if s == 0:
             for copy in tables:
                 copy.wait()
 
         tadpole_row = rows - 1 if s == 0 else rows + current
-        radial = None
-        tadpole = None
-        for k in range(m_count):
-            part = (m - k + m_count) % m_count
-            if k:
-                swaps[k - 1].wait_recv()
-            momenta = momenta_of(part)
-            weight = momenta * (dp / (2.0 * math.pi**2))
-            value = swap[s, part].reshape(2 * extended, width)
-            span = pl.ds(pl.multiple_of(part * width, LANES), width)
-            term = dot3(value * weight, sine_high[span, :], sine_low[span, :])
-            radial = term if radial is None else radial + term
-            line = swap[s, part, 0, pl.ds(tadpole_row, 1), :]
-            term = jnp.sum(weight * momenta * line, axis=1, keepdims=True)
-            tadpole = term if tadpole is None else tadpole + term
-        field_stat = radial[:extended] * inverse_radius
-        field_spec = radial[extended:] * inverse_radius
-        square_stat, square_spec = field_stat * field_stat, field_spec * field_spec
-        sigma_stat = -SUNSET_COUPLING * field_stat * (square_stat - 0.75 * square_spec)
-        sigma_spec = -SUNSET_COUPLING * field_spec * (3.0 * square_stat - 0.25 * square_spec)
-        sigma = jnp.concatenate([sigma_stat * back_factor, sigma_spec * back_factor], axis=0)
-        sigma = dot3(sigma, sine_high[:, own_part], sine_low[:, own_part]) * inverse_momentum
-        group_stat, group_spec = sigma[:rows], sigma[extended : extended + rows]
-        new_stat, new_spec = sigma[rows:extended], sigma[extended + rows :]
-
-        gathered[s, me, pl.ds(0, rows), :] = group_stat
-        extra = []
-        for a in range(5):
-            if a > current:
-                extra.append(zero_row)
-                continue
-            spec = column(1, a)
-            if a < 2:
-                spec = jnp.where(row_time <= times - 2 + a, spec, 0.0)
-            value = group_spec * column(0, a) + group_stat * spec
-            extra.append(-jnp.sum(value, axis=0, keepdims=True))
-        for a in range(2):
-            spec = jnp.where(row_time >= times - 2 + a, column(1, a), 0.0)
-            extra.append(jnp.sum(group_spec * spec, axis=0, keepdims=True))
-        extra.append(jnp.broadcast_to(tadpole * is_last, (1, width)))
-        for k in range(2):
-            for b in range(2):
+        halves = []
+        for piece, (start, size) in enumerate(pieces):
+            radial = None
+            tadpole = None
+            for k in range(m_count):
+                part = (m - k + m_count) % m_count
+                if k:
+                    swaps[piece * (m_count - 1) + k - 1].wait_recv()
+                momenta = momenta_of(part)
+                weight = momenta * (dp / (2.0 * math.pi**2))
+                value = swap[s, part, :, pl.ds(start, size), :].reshape(2 * size, width)
+                span = pl.ds(pl.multiple_of(part * width, LANES), width)
+                term = dot3(value * weight, sine_high[span, :], sine_low[span, :])
+                radial = term if radial is None else radial + term
+                if piece:
+                    line = swap[s, part, 0, pl.ds(tadpole_row, 1), :]
+                    term = jnp.sum(weight * momenta * line, axis=1, keepdims=True)
+                    tadpole = term if tadpole is None else tadpole + term
+            field_stat = radial[:size] * inverse_radius
+            field_spec = radial[size:] * inverse_radius
+            square_stat, square_spec = field_stat * field_stat, field_spec * field_spec
+            sigma_stat = -SUNSET_COUPLING * field_stat * (square_stat - 0.75 * square_spec)
+            sigma_spec = -SUNSET_COUPLING * field_spec * (3.0 * square_stat - 0.25 * square_spec)
+            sigma = jnp.concatenate([sigma_stat * back_factor, sigma_spec * back_factor], axis=0)
+            sigma = dot3(sigma, sine_high[:, own_part], sine_low[:, own_part]) * inverse_momentum
+            halves.append((sigma[:half], sigma[size : size + half]))
+            if piece == 0:
+                gathered[s, me, pl.ds(0, rows), :] = jnp.concatenate(halves[0], axis=0)
+                if s:
+                    drain(s - 1)
+            else:
+                group_stat = jnp.concatenate([halves[0][0], halves[1][0]], axis=0)
+                group_spec = jnp.concatenate([halves[0][1], halves[1][1]], axis=0)
+                new_stat, new_spec = sigma[half:size], sigma[size + half :]
+                extra = []
+                for a in range(5):
+                    if a > current:
+                        extra.append(zero_row)
+                        continue
+                    spec = column(1, a)
+                    if a < 2:
+                        spec = jnp.where(row_time <= times - 2 + a, spec, 0.0)
+                    value = group_spec * column(0, a) + group_stat * spec
+                    extra.append(-jnp.sum(value, axis=0, keepdims=True))
                 for a in range(2):
-                    corner = columns[k, a, pl.ds(rows - 2 + b, 1), :]
-                    extra.append((is_last if k == 0 else -is_last) * corner)
-        gathered[s, me, pl.ds(rows, rows + 2 * TILE), :] = jnp.concatenate([group_spec] + extra, axis=0)
-        for chunk in range(2):
+                    spec = jnp.where(row_time >= times - 2 + a, column(1, a), 0.0)
+                    extra.append(jnp.sum(group_spec * spec, axis=0, keepdims=True))
+                extra.append(jnp.broadcast_to(tadpole * is_last, (1, width)))
+                if s == 0:
+                    for k in range(2):
+                        for b in range(2):
+                            for a in range(2):
+                                corner = columns[k, a, pl.ds(rows - 2 + b, 1), :]
+                                extra.append((is_last if k == 0 else -is_last) * corner)
+                gathered[s, me, pl.ds(rows, rows + len(extra)), :] = jnp.concatenate(
+                    list(halves[1]) + extra, axis=0
+                )
+
             @pl.when(z > 0)
             def _():
-                send(s, me, chunk, 0, {"hist": z - 1}).start()
+                send(s, me, piece, 0, {"hist": z - 1}).start()
 
             @pl.when(z < z_count - 1)
             def _():
-                send(s, me, chunk, 1, {"hist": z + 1}).start()
+                send(s, me, piece, 1, {"hist": z + 1}).start()
 
             for k in range(1, c_count):
-                send(s, me, chunk, 1 + k, {"rep": (c + k) % c_count}).start()
+                send(s, me, piece, 1 + k, {"rep": (c + k) % c_count}).start()
 
         def add_block(q, first):
             group = group_of(q)
@@ -279,8 +309,9 @@
             target = jnp.where(earlier, 0, 1)
             for t in range(width // LANES):
                 lanes = pl.ds(t * LANES, LANES)
-                sig_stat = gathered[s, group, pl.ds(0, rows), lanes]
-                sig_spec = gathered[s, group, pl.ds(rows, rows), lanes]
+                parts = [gathered[s, group, pl.ds(u * half, half), lanes] for u in range(4)]
+                sig_stat = jnp.concatenate([parts[0], parts[2]], axis=0)
+                sig_spec = jnp.concatenate([parts[1], parts[3]], axis=0)
                 mixed = sig_spec if first else jnp.where(earlier, sig_stat, sig_spec)
 
                 def body(i, f, r):
@@ -321,13 +352,7 @@
                 for chunk in range(2):
                     send(s, group, chunk, 1 + k, {"rep": (c + k) % c_count}).wait_recv()
 
-        add_block(0, True)
-        from_others(0)
-        for j in range(1, c_count):
-            add_block(j, False)
-
-        @pl.loop(1, z_count)
-        def _(n):
+        def forward(n):
             zz, below = source(n)
             group = zz * c_count + c
             for chunk in range(2):
@@ -343,12 +368,37 @@
 
                 for k in range(1, c_count):
                     send(s, group, chunk, 1 + k, {"rep": (c + k) % c_count}).start()
-            add_block(n * c_count, False)
+
+        def process(n, first):
+            add_block(n * c_count, first)
             from_others(n)
             for j in range(1, c_count):
                 add_block(n * c_count + j, False)
 
-        total = jnp.sum(gathered[s, :, pl.ds(2 * rows, 2 * TILE), :], axis=0)
+        if s == 0:
+            @pl.loop(1, z_count)
+            def _(n):
+                forward(n)
+
+            process(0, True)
+
+            @pl.loop(1, z_count)
+            def _(n):
+                process(n, False)
+        else:
+            process(0, True)
+
+            @pl.loop(1, z_count + 1)
+            def _(n):
+                @pl.when(n < z_count)
+                def _():
+                    forward(n)
+
+                @pl.when(n > 1)
+                def _():
+                    process(n - 1, False)
+
+        total = jnp.sum(gathered[s, :, pl.ds(2 * rows, 2 * TILE if s == 0 else TILE), :], axis=0)
 
         def total_row(i):
             return total[i : i + 1]
@@ -404,26 +454,16 @@
         for copy in swaps:
             copy.wait_send()
 
-        @pl.loop(0, z_count)
-        def _(n):
-            zz, below = source(n)
-            group = zz * c_count + c
-            for chunk in range(2):
-                @pl.when(((n == 0) | below) & (z < z_count - 1))
-                def _():
-                    send(s, group, chunk, 1, {"hist": z + 1}).wait_send()
-
-                @pl.when(((n == 0) | jnp.logical_not(below)) & (z > 0))
-                def _():
-                    send(s, group, chunk, 0, {"hist": z - 1}).wait_send()
-
-                for k in range(1, c_count):
-                    send(s, group, chunk, 1 + k, {"rep": (c + k) % c_count}).wait_send()
-
+    drain(STEPS - 1)
     for a in range(STEPS + 2):
         for b in range(STEPS + 2):
             newest_stat[a, pl.ds(b, 1), :] = block_stat[(a, b)]
             newest_spec[a, pl.ds(b, 1), :] = block_spec[(a, b)]
+
+
+def pass_on(*refs):
+    for source, target in zip(refs[:4], refs[4:]):
+        target[...] = source[...]
 
 
 def shards(history_stat, history_spec):
@@ -442,7 +482,7 @@
     dma = pltpu.SemaphoreType.DMA
     stream_rows = max(streamed, TILE)
     stream_cols = rows if streamed else TILE
-    return pl.pallas_call(
+    results = pl.pallas_call(
         functools.partial(kernel, sizes),
         out_shape=(
             jax.ShapeDtypeStruct((STEPS, rows, width), F32),
@@ -467,8 +507,8 @@
             dma((2,)),
             dma((groups, 2)),
             dma((SLOTS, 2)),
-            dma((STEPS, m_count)),
-            dma((STEPS, m_count)),
+            dma((STEPS, 2 * m_count)),
+            dma((STEPS, 2 * m_count)),
             dma((groups, 2, 1 + c_count)),
             dma((STEPS, groups, 2)),
         ],
@@ -477,6 +517,13 @@
         ),
         name="steps",
     )(history_stat, history_spec, jnp.asarray(high), jnp.asarray(low))
+    return pl.pallas_call(
+        pass_on,
+        out_shape=tuple(jax.ShapeDtypeStruct(r.shape, r.dtype) for r in results),
+        in_specs=[vmem] * 4,
+        out_specs=(vmem,) * 4,
+        name="pass_on",
+    )(*results)
 
 
 def solution(mesh):

time: 90.2 us -> 75.4 us (0.84)
  Pallas kernels: 83.2 us -> 74.6 us
  local copies, waits for them, and re-layouts: 6.03 us -> 0 us
    pallas_call x1, Pallas kernels: 83.2 us -> 72.8 us  [shards(): pl.pallas_call(functools.partial(kernel, sizes), out_shape=(jax.ShapeDtyp...]
    unnamed x4 -> x0, local copies, waits for them, and re-layouts: 6.03 us -> none
    pallas_call x0 -> x1, Pallas kernels: none -> 1.8 us  [shards(): pl.pallas_call(pass_on, out_shape=tuple((jax.ShapeDtypeStruct(r.shape, r....]
where the time goes in v1:
time: 75.4 us; the launch traced here: 75.3 us
  Pallas kernels  74.6 us (99%)
    pallas_call x1, Pallas kernels, shards(): pl.pallas_call(functools.partial(kernel, sizes), out_shape=(jax.ShapeDtyp...  72.8 us
    pallas_call x1, Pallas kernels, shards(): pl.pallas_call(pass_on, out_shape=tuple((jax.ShapeDtypeStruct(r.shape, r....  1.8 us

profile of v1, /device:TPU:0, one launch (start us, length us, event | category | flops | bytes accessed | tf_op | source)
XLA Modules:
  0.0 75.3 jit_solution(14854887906094665145)
XLA Ops:
  0.6 72.8 %steps.1 = (f32[3,64,256]{2,1,0:T(8,128)}, f32[3,64,256]{2,1,0:T(8,128)}, f32[5,5,256]{2,1,0:T(8,128)}, f32[5,5,256]{2,1,0:T(8,128)}) custom-call(f32[64,512,256]{2,1,0:T(8,128)} %hist_stat.1, f32[64,512,256]{2,1,0:T(8,128)} %hist_spec.1, bf16[512,512]{1,0:T(8,128)(2,1)} %constant.4.clone.sine_high_hbm, bf16[512,512]{1,0:T(8,128)(2,1)} %constant.5.clone.sine_low_hbm), custom_call_target="tpu_custom_call" | custom-call | tf_op jit(solution)/shard_map/steps/pallas_call | solution.py:485
  73.5 1.8 %pass_on.1 = (f32[3,64,256]{2,1,0:T(8,128)}, f32[3,64,256]{2,1,0:T(8,128)}, f32[5,5,256]{2,1,0:T(8,128)}, f32[5,5,256]{2,1,0:T(8,128)}) custom-call(f32[3,64,256]{2,1,0:T(8,128)} %get-tuple-element.8.refs_0_, f32[3,64,256]{2,1,0:T(8,128)} %get-tuple-element.9.refs_1_, f32[5,5,256]{2,1,0:T(8,128)} %get-tuple-element.10.refs_2_, ...), custom_call_target="tpu_custom_call" | custom-call | tf_op jit(solution)/shard_map/pass_on/pallas_call | solution.py:520

commit v2 on v1

--- a/solution.py
+++ b/solution.py
@@ -118,16 +118,19 @@
     def _():
         pl.semaphore_signal(barrier, inc=1, device_id={"hist": z + 1}, device_id_type=MESH)
 
-    @pl.loop(0, groups)
-    def _(q):
-        for copy in keep_copies(q):
-            copy.start()
-        if streamed:
-            @pl.when(q < SLOTS)
-            def _():
-                for copy in stream_copies(q):
-                    copy.start()
-
+    def start_keep(begin, end):
+        @pl.loop(begin, end)
+        def _(q):
+            for copy in keep_copies(q):
+                copy.start()
+            if streamed:
+                @pl.when(q < SLOTS)
+                def _():
+                    for copy in stream_copies(q):
+                        copy.start()
+
+    first_part, second_part = groups // 2, groups // 2 + groups // 4
+    start_keep(0, first_part)
     for copy in cols:
         copy.wait()
     columns[0, 0] = first_cols[0, :, TILE - 2, :]
@@ -376,27 +379,21 @@
                 add_block(n * c_count + j, False)
 
         if s == 0:
-            @pl.loop(1, z_count)
-            def _(n):
+            start_keep(first_part, second_part)
+            forward(1)
+            start_keep(second_part, groups)
+        process(0, True)
+        lag = jnp.where(near > 0, 1, 0) if s else 1
+
+        @pl.loop(1, z_count + 1)
+        def _(n):
+            @pl.when((n > (0 if s else 1)) & (n < z_count))
+            def _():
                 forward(n)
 
-            process(0, True)
-
-            @pl.loop(1, z_count)
-            def _(n):
-                process(n, False)
-        else:
-            process(0, True)
-
-            @pl.loop(1, z_count + 1)
-            def _(n):
-                @pl.when(n < z_count)
-                def _():
-                    forward(n)
-
-                @pl.when(n > 1)
-                def _():
-                    process(n - 1, False)
+            @pl.when((n - lag > 0) & (n - lag < z_count))
+            def _():
+                process(n - lag, False)
 
         total = jnp.sum(gathered[s, :, pl.ds(2 * rows, 2 * TILE if s == 0 else TILE), :], axis=0)
 

time: 75.4 us -> 72.8 us (0.966)
  Pallas kernels: 74.6 us -> 72 us
    pallas_call x1, Pallas kernels: 72.8 us -> 70.2 us  [shards(): pl.pallas_call(functools.partial(kernel, sizes), out_shape=(jax.ShapeDtyp...]
where the time goes in v2:
time: 72.8 us; the launch traced here: 72.6 us
  Pallas kernels  72 us (99%)
    pallas_call x1, Pallas kernels, shards(): pl.pallas_call(functools.partial(kernel, sizes), out_shape=(jax.ShapeDtyp...  70.2 us
    pallas_call x1, Pallas kernels, shards(): pl.pallas_call(pass_on, out_shape=tuple((jax.ShapeDtypeStruct(r.shape, r....  1.8 us

profile of v2, /device:TPU:0, one launch (start us, length us, event | category | flops | bytes accessed | tf_op | source)
XLA Modules:
  0.0 72.6 jit_solution(5756026012812875555)
XLA Ops:
  0.6 70.2 %steps.1 = (f32[3,64,256]{2,1,0:T(8,128)}, f32[3,64,256]{2,1,0:T(8,128)}, f32[5,5,256]{2,1,0:T(8,128)}, f32[5,5,256]{2,1,0:T(8,128)}) custom-call(f32[64,512,256]{2,1,0:T(8,128)} %hist_stat.1, f32[64,512,256]{2,1,0:T(8,128)} %hist_spec.1, bf16[512,512]{1,0:T(8,128)(2,1)} %constant.4.clone.sine_high_hbm, bf16[512,512]{1,0:T(8,128)(2,1)} %constant.5.clone.sine_low_hbm), custom_call_target="tpu_custom_call" | custom-call | tf_op jit(solution)/shard_map/steps/pallas_call | solution.py:482
  70.8 1.8 %pass_on.1 = (f32[3,64,256]{2,1,0:T(8,128)}, f32[3,64,256]{2,1,0:T(8,128)}, f32[5,5,256]{2,1,0:T(8,128)}, f32[5,5,256]{2,1,0:T(8,128)}) custom-call(f32[3,64,256]{2,1,0:T(8,128)} %get-tuple-element.8.refs_0_, f32[3,64,256]{2,1,0:T(8,128)} %get-tuple-element.9.refs_1_, f32[5,5,256]{2,1,0:T(8,128)} %get-tuple-element.10.refs_2_, ...), custom_call_target="tpu_custom_call" | custom-call | tf_op jit(solution)/shard_map/pass_on/pallas_call | solution.py:517
